TPU v7x, 128 devices: a whole 4x4x4 slice. The times are simulated.
128 devices in a mesh: seq: 8 (over z, core), exp: 16 (over x, y).
Axes of the slice: x: 4, y: 4, z: 4, core: 2. Of those that a mesh axis runs over, the one named last changes fastest.
Arguments:
- residual: bfloat16 [16384, 8192], P(('seq', 'exp')), may hold values from -6 to 6
- expert_rows: bfloat16 [8, 16, 16, 24, 8192], P('seq', 'exp'), may hold values from -6 to 6
- expert_ids: int32 [16384, 2], P(('seq', 'exp')), may hold values from 0 to 15, as said below
- expert_slots: int32 [16384, 2], P(('seq', 'exp')), may hold values from 0 to 23, as said below
- combine_weights: float32 [16384, 2], P(('seq', 'exp')), may hold values from 0.1 to 0.9
- norm_gain: float32 [8192], replicated, may hold values from 0.1 to 1.9
- in_weight: bfloat16 [8192, 8192], P(None, 'exp'), may hold values from -0.0625 to 0.0625
- conv_weight: float32 [4, 8192], P(None, 'exp'), may hold values from -3 to 3
- conv_bias: float32 [8192], P('exp'), may hold values from -0.5 to 0.5
- bc_weight: bfloat16 [8192, 128], P('exp'), may hold values from -0.00390625 to 0.00390625
- dt_weight: bfloat16 [8192, 128], P('exp'), may hold values from -0.0625 to 0.0625
- dt_bias: float32 [128], P('exp'), may hold values from -2 to 0.5
- decay_log: float32 [128], P('exp'), may hold values from -14 to -3.2
- skip_gain: float32 [128], P('exp'), may hold values from -1 to 3
Outputs:
- scan_output: bfloat16 [16384, 8192], P('seq', 'exp')
Inputs may be any that keep to these rules, and one draw needn't show every extreme that they name: `expert_ids`: A token's two ids differ. The tokens of one device name no expert more than 24 times, and in each span one expert is named exactly 24 times by the tokens of every device of the span. `expert_slots`: A token's slot at its k-th expert counts the earlier (token, k) pairs of the same device, in row-major order, that name the same expert.
All inputs are finite; a program needn't handle non-finite values.
Results may differ from a plain program's by a relative error of at most 0.0074.
Values may be sent and summed in bfloat16 or wider, within the bound.
No kernel may reach another device: no remote copies, remote signals or barrier semaphores. Data moves between devices by JAX's collectives and lax.ppermute only.
A program may use at most 320 MiB of HBM per device.

v0:
```python
import jax
import jax.numpy as jnp
from jax import lax
from jax.sharding import PartitionSpec as P

TOPK = 2
KCONV = 4
HEAD = 64
NSTATE = 64
STRETCH = 256


def passed_along(value, axis, steps):
    count = lax.axis_size(axis)
    leading, last = (max(0, -steps), min(count, count - steps))
    return lax.ppermute(value, axis, [(source, source + steps) for source in range(leading, last)])


def block_terms(b_rows, c_rows, steps_dt, decays, values):
    running = jnp.cumsum(decays, axis=0)
    scores = jnp.dot(c_rows, b_rows.T, preferred_element_type=jnp.float32)
    length = running.shape[0]
    causal = (jnp.arange(length)[:, None] >= jnp.arange(length)[None, :])[:, :, None]
    decay_gap = jnp.where(causal, running[:, None, :] - running[None, :, :], 0.0)
    mixing = jnp.where(
        causal, jnp.exp(decay_gap) * scores[:, :, None] * steps_dt[None, :, :], 0.0
    ).astype(jnp.bfloat16)
    inside = jnp.einsum("tsh,shp->thp", mixing, values, preferred_element_type=jnp.float32)
    carried = jnp.exp(running[-1][None, :] - running) * steps_dt
    states = jnp.einsum(
        "sn,shp->hnp",
        b_rows.astype(jnp.float32),
        carried[:, :, None] * values.astype(jnp.float32),
        precision=lax.Precision.HIGHEST,
    )
    return (running, inside, states, jnp.exp(running[-1]))


def shards(
    residual,
    expert_rows,
    expert_ids,
    expert_slots,
    combine_weights,
    norm_gain,
    in_weight,
    conv_weight,
    conv_bias,
    bc_weight,
    dt_weight,
    dt_bias,
    decay_log,
    skip_gain,
):
    own_rows, width = residual.shape
    returned = lax.all_to_all(expert_rows, "exp", split_axis=2, concat_axis=1, tiled=True)
    capacity = returned.shape[3]
    buffers = returned.reshape(returned.shape[1] * capacity, width)
    picked = jnp.take(buffers, expert_ids * capacity + expert_slots, axis=0)
    mixture = jnp.zeros((own_rows, width), jnp.float32)
    for column in range(TOPK):
        mixture = mixture + combine_weights[:, column][:, None] * picked[:, column].astype(
            jnp.float32
        )
    stream = residual.astype(jnp.float32) + mixture
    factor = lax.rsqrt(jnp.mean(stream * stream, axis=1, keepdims=True) + 1e-06)
    normed = (stream * factor * norm_gain[None, :]).astype(jnp.bfloat16)
    group_rows = own_rows * lax.axis_size("exp")
    local_width = in_weight.shape[1]
    x_in = jnp.dot(
        lax.all_gather(normed, "exp", axis=0, tiled=True),
        in_weight,
        preferred_element_type=jnp.float32,
    ).astype(jnp.bfloat16)
    rim_rows = passed_along(x_in[group_rows - (KCONV - 1) :], "seq", 1)
    padded = jnp.concatenate([rim_rows, x_in], axis=0)
    filtered = jnp.zeros((group_rows, local_width), jnp.float32) + conv_bias[None, :]
    for tap in range(KCONV):
        filtered = filtered + conv_weight[tap][None, :] * padded[tap : tap + group_rows].astype(
            jnp.float32
        )
    activated = jax.nn.silu(filtered).astype(jnp.bfloat16)
    state_part = jnp.dot(activated, bc_weight, preferred_element_type=jnp.float32)
    rate_part = jnp.dot(activated, dt_weight, preferred_element_type=jnp.float32)
    state_proj, dt_raw = lax.psum((state_part, rate_part), "exp")
    heads_here = local_width // HEAD
    first_head = lax.axis_index("exp") * heads_here
    steps_dt = jax.nn.softplus(
        lax.dynamic_slice_in_dim(dt_raw, first_head, heads_here, 1) + dt_bias[None, :]
    )
    decays = -jnp.exp(decay_log)[None, :] * steps_dt
    b_all = state_proj[:, :NSTATE].astype(jnp.bfloat16)
    c_all = state_proj[:, NSTATE:].astype(jnp.bfloat16)
    blocks = group_rows // STRETCH
    c_blocks = c_all.reshape(blocks, STRETCH, NSTATE)
    value_blocks = activated.reshape(blocks, STRETCH, heads_here, HEAD)

    def advance(carry, inputs):
        local_states, prefix_decay = carry
        b_rows, c_rows, block_dt, block_decays, values = inputs
        running, inside, states, total = block_terms(b_rows, c_rows, block_dt, block_decays, values)
        return (
            (total[:, None, None] * local_states + states, prefix_decay * total),
            (running, inside, local_states, prefix_decay),
        )

    start_carry = (
        jnp.zeros((heads_here, NSTATE, HEAD), jnp.float32),
        jnp.ones((heads_here,), jnp.float32),
    )
    (final_states, device_decay), (runnings, insides, starts, prefixes) = lax.scan(
        advance,
        start_carry,
        (
            b_all.reshape(blocks, STRETCH, NSTATE),
            c_blocks,
            steps_dt.reshape(blocks, STRETCH, heads_here),
            decays.reshape(blocks, STRETCH, heads_here),
            value_blocks,
        ),
    )
    empty_states = jnp.zeros((heads_here, NSTATE, HEAD), jnp.float32)

    def relay_turn(turn, carried):
        incoming, outgoing = carried
        incoming = passed_along(outgoing, "seq", 1)
        return (incoming, device_decay[:, None, None] * incoming + final_states)

    incoming, outgoing_last = lax.fori_loop(
        0, lax.axis_size("seq") - 1, relay_turn, (empty_states, final_states)
    )
    entering = starts + prefixes[:, :, None, None] * incoming[None]
    across = jnp.exp(runnings)[:, :, :, None] * jnp.einsum(
        "btn,bhnp->bthp", c_blocks.astype(jnp.float32), entering, precision=lax.Precision.HIGHEST
    )
    output = insides + across + skip_gain[None, None, :, None] * value_blocks.astype(jnp.float32)
    return output.astype(jnp.bfloat16).reshape(group_rows, local_width)


def solution(mesh):
    placed = (
        P(("seq", "exp"), None),
        P("seq", "exp", None, None, None),
        P(("seq", "exp"), None),
        P(("seq", "exp"), None),
        P(("seq", "exp"), None),
        P(),
        P(None, "exp"),
        P(None, "exp"),
        P("exp"),
        P("exp", None),
        P("exp", None),
        P("exp"),
        P("exp"),
        P("exp"),
    )
    return jax.shard_map(
        shards, mesh=mesh, in_specs=placed, out_specs=P("seq", "exp"), check_vma=False
    )
```

profile of v0, /device:TPU:1, one launch (start us, length us, event | category | flops | bytes accessed | tf_op | source)
XLA Modules:
  0.0 613.7 jit_solution(3130771036729045118)
XLA Ops:
  6.5 7.8 %all-to-all-start = ((bf16[1,1,16,24,8192]{4,3,1,0,2:T(8,128)(2,1)}), bf16[1,1,16,24,8192]{4,3,1,0,2:T(8,128)(2,1)}, u32[]{:S(2)}, u32[]{:S(2)}) async-start(bf16[1,1,16,24,8192]{4,3,1,0,2:T(8,128)(2,1)} %bitcast.113), calls=%async_computation | async-start | bytes 12582912 | tf_op jit(solution)/shard_map/all_to_all | solution.py:56
  14.7 98.2 %all-to-all-done = bf16[1,1,16,24,8192]{4,3,1,0,2:T(8,128)(2,1)} async-done(((bf16[1,1,16,24,8192]{4,3,1,0,2:T(8,128)(2,1)}), bf16[1,1,16,24,8192]{4,3,1,0,2:T(8,128)(2,1)}, u32[]{:S(2)}, u32[]{:S(2)}) %all-to-all-start) | async-done | bytes 6291488 | tf_op jit(solution)/shard_map/all_to_all | solution.py:56
  112.9 12.6 %gather_fusion = bf16[256,8192]{1,0:T(8,128)(2,1)} fusion(bf16[384,8192]{1,0:T(8,128)(2,1)} %bitcast.3, s32[1024]{0:T(1024)S(1)} %pad_clamp_fusion), kind=kCustom, calls=%fused_computation | custom fusion | bytes 8389632 | tf_op jit(solution)/shard_map/jit(_take)/gather | solution.py:59
  125.5 7.6 %reshape.94 = bf16[128,2,8192]{2,1,0:T(2,128)(2,1)} reshape(bf16[256,8192]{1,0:T(8,128)(2,1)} %gather_fusion) | data formatting | bytes 8388608 | tf_op jit(solution)/shard_map/jit(_take)/gather | solution.py:59
  133.1 7.2 %copy_select_fusion = bf16[128,2,8192]{2,0,1:T(8,128)(2,1)S(1)} fusion(bf16[128,2,8192]{2,1,0:T(2,128)(2,1)} %reshape.94, pred[128,2]{0,1:T(4,128)(4,1)S(1)} %get-tuple-element.250), kind=kLoop, calls=%fused_computation.47 | loop fusion | flops 2097152 | bytes 8388864 | tf_op jit(solution)/shard_map/jit(_take)/select_n | solution.py:59
  140.3 1.4 multiply_reduce_fusion
  141.7 3.0 multiply_convert_fusion.1
  144.9 206.7 %all-gather.2.cloned.1.call-done = bf16[2048,8192]{1,0:T(8,128)(2,1)} async-done(((bf16[128,8192]{1,0:T(8,128)(2,1)}), bf16[2048,8192]{1,0:T(8,128)(2,1)}) %all-gather.2.cloned.1.call-update) | async-done | bytes 33554448 | tf_op jit(solution)/shard_map/all_gather | solution.py:71
  351.6 23.7 %convolution_convert_fusion = bf16[2048,512]{1,0:T(8,128)(2,1)S(1)} fusion(bf16[2048,8192]{1,0:T(8,128)(2,1)} %all-gather.2.cloned.1.call-done, bf16[8192,512]{1,0:T(8,128)(2,1)} %param.24), kind=kOutput, calls=%fused_computation.52 | convolution fusion | flops 17180917760 | bytes 44040192 | tf_op jit(solution)/shard_map/dot_general | solution.py:70
  375.3 1.3 copy-done.4
  376.7 3.9 collective-permute-start.1
  381.3 6.0 multiply_convert_fusion
  387.3 1.8 fusion.34
  389.1 1.7 fusion.35
  390.8 3.6 reshape.109
  394.5 4.0 copy.57
  398.5 75.8 %all-reduce.4 = bf16[2048,128]{1,0:T(8,128)(2,1)S(1)} all-reduce(f32[2048,128]{1,0:T(8,128)} %fusion.35), channel_id=1, replica_groups=mesh['seq'=8,'exp'=16] {'exp'}, use_global_device_ids=true, to_apply=%region_1.2 | all-reduce | flops 262144 | bytes 1572864 | tf_op jit(solution)/shard_map/psum | solution.py:85
  474.4 1.0 fusion.32
  475.4 1.2 copy.58
  476.6 1.0 broadcast_multiply_fusion
  477.6 38.5 %while.34 = (s32[]{:T(128)}, f32[8,64,64]{1,2,0:T(8,128)S(1)}, f32[8]{0:T(128)S(1)}, f32[8,256,8]{1,2,0:T(8,128)}, f32[8,256,8,64]{1,3,2,0:T(8,128)}, /*index=5*...) while((s32[]{:T(128)}, f32[8,64,64]{1,2,0:T(8,128)S(1)}, ...), condition=%wide.region_6.7_spmd.clone, body=%wide.region_3.6_spmd.clone.sunk | while | flops 180033568 | bytes 2758157 | solution.py:111
  479.0 1.6 fusion.62
  480.5 0.7 bitcast_dynamic-update-slice_fusion.5
  481.8 0.7 bitcast_dynamic-update-slice_fusion.4
  483.8 1.6 fusion.62
  485.3 0.7 bitcast_dynamic-update-slice_fusion.5
  486.6 0.7 bitcast_dynamic-update-slice_fusion.4
  488.6 1.6 fusion.62
  490.2 0.7 bitcast_dynamic-update-slice_fusion.5
  493.4 1.6 fusion.62
  495.0 0.7 bitcast_dynamic-update-slice_fusion.5
  496.2 0.7 bitcast_dynamic-update-slice_fusion.4
  498.2 1.6 fusion.62
  499.8 0.7 bitcast_dynamic-update-slice_fusion.5
  501.0 0.7 bitcast_dynamic-update-slice_fusion.4
  503.0 1.6 fusion.62
  504.6 0.7 bitcast_dynamic-update-slice_fusion.5
  505.8 0.7 bitcast_dynamic-update-slice_fusion.4
  507.8 1.6 fusion.62
  509.4 0.7 bitcast_dynamic-update-slice_fusion.5
  512.6 1.5 fusion.62
  514.2 0.7 bitcast_dynamic-update-slice_fusion.5
  515.4 0.7 bitcast_dynamic-update-slice_fusion.4
  516.3 71.0 %while.33 = (s32[]{:T(128)}, f32[8,64,64]{2,1,0:T(8,128)}, f32[8,64,64]{2,1,0:T(8,128)S(1)}, f32[8]{0:T(128)S(1)}, f32[8,64,64]{2,1,0:T(8,128)S(1)}, /*index=5*/s32[]{:T(128)}) while((s32[]{:T(128)}, f32[8,64,64]{2,1,0:T(8,128)}, f32[8,64,64]{2,1,0:T(8,128)S(1)}, f32[8]{0:T(128)S(1)}, f32[8,64,64]{2,1,0:T(8,128)S(1)}, ...), condition=%wide.region_8.9_spmd, body=%wide.region_7.8_spmd.sunk | while | flops 65538 | bytes 1441961 | solution.py:129
  516.3 16.8 %collective-permute-start = (f32[8,64,64]{2,1,0:T(8,128)S(1)}, f32[8,64,64]{2,1,0:T(8,128)S(1)}, u32[]{:S(2)}, u32[]{:S(2)}) collective-permute-start(f32[8,64,64]{2,1,0:T(8,128)S(1)} %get-tuple-element.428), channel_id=1, source_target_pairs={{0,16},{16,32},{32,48},{48,64},{64,80},{80,96},{96,112},{1,17},{17... | collective-permute-start | bytes 393224 | tf_op jit(solution)/shard_map/while/body/eval_jaxpr/ppermute | solution.py:16
  533.1 3.3 collective-permute-done
  537.1 4.4 collective-permute-start
  541.4 3.3 collective-permute-done
  545.4 4.4 collective-permute-start
  549.8 3.3 collective-permute-done
  553.8 4.4 collective-permute-start
  558.2 3.3 collective-permute-done
  562.2 4.4 collective-permute-start
  566.6 3.3 collective-permute-done
  570.6 4.4 collective-permute-start
  575.0 3.3 collective-permute-done
  578.9 4.4 collective-permute-start
  583.3 3.3 collective-permute-done
  587.3 1.1 copy.61
  588.4 1.8 multiply_add_fusion.1
  590.3 1.8 fusion.36
  592.5 2.8 add_convert_fusion
  595.3 5.1 copy.67
  600.4 6.4 %reshape.108 = bf16[2048,512]{1,0:T(8,128)(2,1)} reshape(bf16[8,256,8,64]{3,2,1,0:T(8,128)(2,1)} %copy.67) | data formatting | bytes 4194304 | tf_op jit(solution)/shard_map/reshape | solution.py:137
  (181 shorter events, 22.4 us)
Async XLA Ops:
  6.5 380.8 %copy-start = (bf16[512,128]{1,0:T(8,128)(2,1)S(1)}, bf16[512,128]{1,0:T(8,128)(2,1)}, u32[]{:S(2)}) copy-start(bf16[512,128]{1,0:T(8,128)(2,1)} %param.28) | copy-start | bytes 393220
  6.5 7.8 %copy-start.10 = (s32[128,2]{0,1:T(2,128)S(1)}, s32[128,2]{0,1:T(2,128)}, u32[]{:S(2)}) copy-start(s32[128,2]{0,1:T(2,128)} %param.21) | copy-start | bytes 3076
  6.5 7.8 %copy-start.11 = (s32[128,2]{0,1:T(2,128)S(1)}, s32[128,2]{0,1:T(2,128)}, u32[]{:S(2)}) copy-start(s32[128,2]{0,1:T(2,128)} %param.20) | copy-start | bytes 3076
  6.5 8.1 %copy-start.12 = (f32[128,2]{0,1:T(2,128)S(1)}, f32[128,2]{0,1:T(2,128)}, u32[]{:S(2)}) copy-start(f32[128,2]{0,1:T(2,128)} %param.22) | copy-start | bytes 3076
  6.5 106.4 %all-to-all-start = ((bf16[1,1,16,24,8192]{4,3,1,0,2:T(8,128)(2,1)}), bf16[1,1,16,24,8192]{4,3,1,0,2:T(8,128)(2,1)}, u32[]{:S(2)}, u32[]{:S(2)}) async-start(bf16[1,1,16,24,8192]{4,3,1,0,2:T(8,128)(2,1)} %bitcast.113), calls=%async_computation | async-start | bytes 12582912 | tf_op jit(solution)/shard_map/all_to_all | solution.py:56
  14.3 337.3 %all-gather.2.cloned.1.call-start = ((), (), s32[]{:S(2)}) async-start(), calls=%async_computation.1 | async-start | bytes 35651584 | tf_op jit(solution)/shard_map/all_gather | solution.py:71
  133.1 7.2 %copy-start.2 = (bf16[128,8192]{1,0:T(8,128)(2,1)S(1)}, bf16[128,8192]{1,0:T(8,128)(2,1)}, u32[]{:S(2)}) copy-start(bf16[128,8192]{1,0:T(8,128)(2,1)} %param.18) | copy-start | bytes 6291460
  140.3 1.4 copy-start.7
  141.7 3.1 copy-start.8
  144.8 331.9 %all-reduce.3.cloned.1.call-start = ((), (), s32[]{:S(2)}) async-start(), calls=%async_computation.2 | async-start | bytes 2097152 | tf_op jit(solution)/shard_map/psum | solution.py:85
  144.8 235.7 %copy-start.15 = (f32[8]{0:T(128)S(1)}, f32[8]{0:T(128)}, u32[]{:S(2)}) copy-start(f32[8]{0:T(128)} %param.30) | copy-start | bytes 100
  144.8 236.5 %copy-start.9 = (f32[512]{0:T(512)S(1)}, f32[512]{0:T(512)}, u32[]{:S(2)}) copy-start(f32[512]{0:T(512)} %param.26) | copy-start | bytes 6148
  375.3 1.3 copy-start.4
  376.7 4.6 collective-permute-start.1
  381.3 7.8 %copy-start.5 = (bf16[512,128]{1,0:T(8,128)(2,1)S(1)}, bf16[512,128]{1,0:T(8,128)(2,1)}, u32[]{:S(2)}) copy-start(bf16[512,128]{1,0:T(8,128)(2,1)} %param.27) | copy-start | bytes 393220
  394.5 82.1 %copy-start.13 = (f32[8]{0:T(128)S(1)}, f32[8]{0:T(128)}, u32[]{:S(2)}) copy-start(f32[8]{0:T(128)} %param.29) | copy-start | bytes 100
  516.3 20.1 %collective-permute-start = (f32[8,64,64]{2,1,0:T(8,128)S(1)}, f32[8,64,64]{2,1,0:T(8,128)S(1)}, u32[]{:S(2)}, u32[]{:S(2)}) collective-permute-start(f32[8,64,64]{2,1,0:T(8,128)S(1)} %get-tuple-element.428), channel_id=1, source_target_pairs={{0,16},{16,32},{32,48},{48,64},{64,80},{80,96},{96,112},{1,17},{17... | collective-permute-start | bytes 393224 | tf_op jit(solution)/shard_map/while/body/eval_jaxpr/ppermute | solution.py:16
  536.4 0.7 copy-start.1
  537.1 7.7 %collective-permute-start = (f32[8,64,64]{2,1,0:T(8,128)S(1)}, f32[8,64,64]{2,1,0:T(8,128)S(1)}, u32[]{:S(2)}, u32[]{:S(2)}) collective-permute-start(f32[8,64,64]{2,1,0:T(8,128)S(1)} %get-tuple-element.428), channel_id=1, source_target_pairs={{0,16},{16,32},{32,48},{48,64},{64,80},{80,96},{96,112},{1,17},{17... | collective-permute-start | bytes 393224 | tf_op jit(solution)/shard_map/while/body/eval_jaxpr/ppermute | solution.py:16
  544.7 0.7 copy-start.1
  545.4 7.7 %collective-permute-start = (f32[8,64,64]{2,1,0:T(8,128)S(1)}, f32[8,64,64]{2,1,0:T(8,128)S(1)}, u32[]{:S(2)}, u32[]{:S(2)}) collective-permute-start(f32[8,64,64]{2,1,0:T(8,128)S(1)} %get-tuple-element.428), channel_id=1, source_target_pairs={{0,16},{16,32},{32,48},{48,64},{64,80},{80,96},{96,112},{1,17},{17... | collective-permute-start | bytes 393224 | tf_op jit(solution)/shard_map/while/body/eval_jaxpr/ppermute | solution.py:16
  553.1 0.7 copy-start.1
  553.8 7.7 %collective-permute-start = (f32[8,64,64]{2,1,0:T(8,128)S(1)}, f32[8,64,64]{2,1,0:T(8,128)S(1)}, u32[]{:S(2)}, u32[]{:S(2)}) collective-permute-start(f32[8,64,64]{2,1,0:T(8,128)S(1)} %get-tuple-element.428), channel_id=1, source_target_pairs={{0,16},{16,32},{32,48},{48,64},{64,80},{80,96},{96,112},{1,17},{17... | collective-permute-start | bytes 393224 | tf_op jit(solution)/shard_map/while/body/eval_jaxpr/ppermute | solution.py:16
  561.5 0.7 copy-start.1
  562.2 7.7 %collective-permute-start = (f32[8,64,64]{2,1,0:T(8,128)S(1)}, f32[8,64,64]{2,1,0:T(8,128)S(1)}, u32[]{:S(2)}, u32[]{:S(2)}) collective-permute-start(f32[8,64,64]{2,1,0:T(8,128)S(1)} %get-tuple-element.428), channel_id=1, source_target_pairs={{0,16},{16,32},{32,48},{48,64},{64,80},{80,96},{96,112},{1,17},{17... | collective-permute-start | bytes 393224 | tf_op jit(solution)/shard_map/while/body/eval_jaxpr/ppermute | solution.py:16
  569.9 0.7 copy-start.1
  570.6 7.7 %collective-permute-start = (f32[8,64,64]{2,1,0:T(8,128)S(1)}, f32[8,64,64]{2,1,0:T(8,128)S(1)}, u32[]{:S(2)}, u32[]{:S(2)}) collective-permute-start(f32[8,64,64]{2,1,0:T(8,128)S(1)} %get-tuple-element.428), channel_id=1, source_target_pairs={{0,16},{16,32},{32,48},{48,64},{64,80},{80,96},{96,112},{1,17},{17... | collective-permute-start | bytes 393224 | tf_op jit(solution)/shard_map/while/body/eval_jaxpr/ppermute | solution.py:16
  578.2 0.7 copy-start.1
  578.9 7.7 %collective-permute-start = (f32[8,64,64]{2,1,0:T(8,128)S(1)}, f32[8,64,64]{2,1,0:T(8,128)S(1)}, u32[]{:S(2)}, u32[]{:S(2)}) collective-permute-start(f32[8,64,64]{2,1,0:T(8,128)S(1)} %get-tuple-element.428), channel_id=1, source_target_pairs={{0,16},{16,32},{32,48},{48,64},{64,80},{80,96},{96,112},{1,17},{17... | collective-permute-start | bytes 393224 | tf_op jit(solution)/shard_map/while/body/eval_jaxpr/ppermute | solution.py:16
  586.6 0.7 copy-start.1
  590.2 1.9 copy-start.6
  590.3 2.2 copy-start.3
  590.3 2.2 copy-start.14
Sparse Core Ops, SparseCore 0:
  144.9 206.6 all-gather.1
  389.3 86.6 all-reduce.2
where the time goes:
time: 615 us; the launch traced here: 614 us
  waiting for transfers between devices  329 us (53%)
  blocking collectives  75.8 us (12%)
  starting transfers between devices  54.8 us (9%)
  local copies, waits for them, and re-layouts  52.2 us (8%)
  matrix products  46.7 us (8%)
  other arithmetic  41.4 us (7%)
  between operations  13.8 us (2%)
    all_gather x1, waiting for transfers between devices, shards(): lax.all_gather(normed, 'exp', axis=0, tiled=True)  207 us
    all_to_all x1, waiting for transfers between devices, shards(): lax.all_to_all(expert_rows, 'exp', split_axis=2, concat_axis=1, tiled=True)  98.2 us
    psum x1, blocking collectives, shards(): state_proj, dt_raw = lax.psum((state_part, rate_part), 'exp')  75.8 us
    ppermute x8, starting transfers between devices, passed_along(): lax.ppermute(value, axis, [(source, source + steps) for source in range(l...  46.9 us
    dot_general x1, matrix products, shards(): jnp.dot(lax.all_gather(normed, 'exp', axis=0, tiled=True), in_weight, pre...  23.7 us
    ppermute x8, waiting for transfers between devices, passed_along(): lax.ppermute(value, axis, [(source, source + steps) for source in range(l...  23.7 us
    gather x2, local copies, waits for them, and re-layouts, shards(): picked = jnp.take(buffers, expert_ids * capacity + expert_slots, axis=0)  20.2 us
    dot_general x8, matrix products, block_terms(): jnp.einsum('tsh,shp->thp', mixing, values, preferred_element_type=jnp.flo...  12.5 us
  transfers between devices with their start and end apart: 11, of which 10 were waited for; matrix products, arithmetic and copies ran while one was open for 2% of the time, Pallas kernels for 0%

commit v1 on v0

v1 whole, which is shorter than its diff:
```python
import jax
import jax.numpy as jnp
from jax import lax
from jax.experimental import pallas as pl
from jax.experimental.pallas import tpu as pltpu
from jax.sharding import PartitionSpec as P

KCONV = 4
HEAD = 64
NSTATE = 64
STRETCH = 256
PAIR = 2 * HEAD
F32 = jnp.float32
BF16 = jnp.bfloat16
CHUNKS = 2


def mm(a, b):
    return jnp.dot(a, b, preferred_element_type=F32)


def combine_body(hi_ref, lo_ref, rows_ref, residual_ref, gain_ref, out_ref, stream, square):
    step = pl.program_id(0)
    part = rows_ref.shape[1]
    rows = rows_ref[...]
    value = residual_ref[...].astype(F32) + (mm(hi_ref[...], rows) + mm(lo_ref[...], rows))
    stream[:, pl.ds(pl.multiple_of(step * part, part), part)] = value
    total = jnp.sum(value * value, axis=1, keepdims=True)

    @pl.when(step == 0)
    def _():
        square[...] = total

    @pl.when(step > 0)
    def _():
        square[...] = square[...] + total

    @pl.when(step == pl.num_programs(0) - 1)
    def _():
        width = stream.shape[1]
        factor = lax.rsqrt(square[...] * (1.0 / width) + 1e-06)
        for left in range(0, width, part):
            cut = slice(left, left + part)
            out_ref[:, cut] = (stream[:, cut] * factor * gain_ref[:, cut]).astype(BF16)


def combine(hi, lo, rows, residual, gain):
    own, slots = hi.shape
    width = rows.shape[1]
    part = 1024
    return pl.pallas_call(
        combine_body,
        grid=(width // part,),
        in_specs=[
            pl.BlockSpec((own, slots), lambda i: (0, 0)),
            pl.BlockSpec((own, slots), lambda i: (0, 0)),
            pl.BlockSpec((slots, part), lambda i: (0, i)),
            pl.BlockSpec((own, part), lambda i: (0, i)),
            pl.BlockSpec((1, width), lambda i: (0, 0)),
        ],
        out_specs=pl.BlockSpec((own, width), lambda i: (0, 0)),
        out_shape=jax.ShapeDtypeStruct((own, width), BF16),
        scratch_shapes=[pltpu.VMEM((own, width), F32), pltpu.VMEM((own, 1), F32)],
        name="combine",
    )(hi, lo, rows, residual, gain)


def by_pair(first, second, shape):
    lane = lax.broadcasted_iota(jnp.int32, shape, 1)
    return jnp.where(lane < HEAD, jnp.broadcast_to(first, shape), jnp.broadcast_to(second, shape))


def split(value):
    high = value.astype(BF16)
    return high, (value - high.astype(F32)).astype(BF16)


def states_body(values_ref, b_ref, row_ref, dt_ref, col_ref, starts_ref, final_ref, carry):
    step = pl.program_id(0)

    @pl.when(step == 0)
    def _():
        carry[...] = jnp.zeros_like(carry)

    starts_ref[0] = carry[...]
    row = row_ref[...]
    carried = jnp.exp(row[:, STRETCH - 1 :] - row) * dt_ref[...]
    total = jnp.exp(col_ref[STRETCH - 1 :, :])
    b = b_ref[...].astype(F32)
    for pair in range(values_ref.shape[1] // PAIR):
        cut = slice(pair * PAIR, (pair + 1) * PAIR)
        pair_values = values_ref[:, cut]
        sums = []
        for head in (2 * pair, 2 * pair + 1):
            high, low = split(b * carried[head : head + 1, :])
            sums.append(mm(high, pair_values) + mm(low, pair_values))
        fresh = by_pair(sums[0], sums[1], (NSTATE, PAIR))
        keep = by_pair(
            total[:, 2 * pair : 2 * pair + 1], total[:, 2 * pair + 1 : 2 * pair + 2], (1, PAIR)
        )
        carry[:, cut] = keep * carry[:, cut] + fresh

    @pl.when(step == pl.num_programs(0) - 1)
    def _():
        final_ref[...] = carry[...]


def states_of(values, b_t, row, dt_row, col):
    rows, width = values.shape
    blocks = rows // STRETCH
    heads = row.shape[0]
    return pl.pallas_call(
        states_body,
        grid=(blocks,),
        in_specs=[
            pl.BlockSpec((STRETCH, width), lambda i: (i, 0)),
            pl.BlockSpec((NSTATE, STRETCH), lambda i: (0, i)),
            pl.BlockSpec((heads, STRETCH), lambda i: (0, i)),
            pl.BlockSpec((heads, STRETCH), lambda i: (0, i)),
            pl.BlockSpec((STRETCH, heads), lambda i: (i, 0)),
        ],
        out_specs=[
            pl.BlockSpec((1, NSTATE, width), lambda i: (i, 0, 0)),
            pl.BlockSpec((NSTATE, width), lambda i: (0, 0)),
        ],
        out_shape=[
            jax.ShapeDtypeStruct((blocks, NSTATE, width), F32),
            jax.ShapeDtypeStruct((NSTATE, width), F32),
        ],
        scratch_shapes=[pltpu.VMEM((NSTATE, width), F32)],
        name="states",
    )(values, b_t, row, dt_row, col)


def inside_body(values_ref, b_ref, c_ref, row_ref, dt_ref, col_ref, starts_ref, skip_ref, out_ref):
    scores = mm(c_ref[...], b_ref[...])
    square = (STRETCH, STRETCH)
    causal = lax.broadcasted_iota(jnp.int32, square, 0) >= lax.broadcasted_iota(jnp.int32, square, 1)
    scores = jnp.where(causal, scores, 0.0)
    row = row_ref[...]
    col = col_ref[...]
    dt_row = dt_ref[...]
    grown = jnp.exp(col)
    c = c_ref[...]
    for pair in range(values_ref.shape[1] // PAIR):
        cut = slice(pair * PAIR, (pair + 1) * PAIR)
        pair_values = values_ref[:, cut]
        sums = []
        for head in (2 * pair, 2 * pair + 1):
            gap = jnp.minimum(col[:, head : head + 1] - row[head : head + 1, :], 0.0)
            mixing = (jnp.exp(gap) * scores * dt_row[head : head + 1, :]).astype(BF16)
            sums.append(mm(mixing, pair_values))
        inside = by_pair(sums[0], sums[1], (STRETCH, PAIR))
        high, low = split(starts_ref[0, :, cut])
        across = by_pair(
            grown[:, 2 * pair : 2 * pair + 1],
            grown[:, 2 * pair + 1 : 2 * pair + 2],
            (STRETCH, PAIR),
        ) * (mm(c, high) + mm(c, low))
        out_ref[:, cut] = inside + across + skip_ref[:, cut] * pair_values.astype(F32)


def inside_of(values, b_t, c, row, dt_row, col, starts, skip):
    rows, width = values.shape
    heads = row.shape[0]
    return pl.pallas_call(
        inside_body,
        grid=(rows // STRETCH,),
        in_specs=[
            pl.BlockSpec((STRETCH, width), lambda i: (i, 0)),
            pl.BlockSpec((NSTATE, STRETCH), lambda i: (0, i)),
            pl.BlockSpec((STRETCH, NSTATE), lambda i: (i, 0)),
            pl.BlockSpec((heads, STRETCH), lambda i: (0, i)),
            pl.BlockSpec((heads, STRETCH), lambda i: (0, i)),
            pl.BlockSpec((STRETCH, heads), lambda i: (i, 0)),
            pl.BlockSpec((1, NSTATE, width), lambda i: (i, 0, 0)),
            pl.BlockSpec((1, width), lambda i: (0, 0)),
        ],
        out_specs=pl.BlockSpec((STRETCH, width), lambda i: (i, 0)),
        out_shape=jax.ShapeDtypeStruct((rows, width), F32),
        cost_estimate=pl.CostEstimate(
            flops=40 * rows * STRETCH * heads * HEAD,
            transcendentals=rows * STRETCH * heads,
            bytes_accessed=8 * rows * width,
        ),
        name="inside",
    )(values, b_t, c, row, dt_row, col, starts, skip)


def finish_body(partial_ref, c_ref, long_ref, incoming_ref, out_ref):
    grown = jnp.exp(long_ref[...])
    c = c_ref[...]
    for pair in range(partial_ref.shape[1] // PAIR):
        cut = slice(pair * PAIR, (pair + 1) * PAIR)
        high, low = split(incoming_ref[:, cut])
        scale = by_pair(
            grown[:, 2 * pair : 2 * pair + 1],
            grown[:, 2 * pair + 1 : 2 * pair + 2],
            (STRETCH, PAIR),
        )
        out_ref[:, cut] = (partial_ref[:, cut] + scale * (mm(c, high) + mm(c, low))).astype(BF16)


def finish(partial, c, long_col, incoming):
    rows, width = partial.shape
    heads = long_col.shape[1]
    return pl.pallas_call(
        finish_body,
        grid=(rows // STRETCH,),
        in_specs=[
            pl.BlockSpec((STRETCH, width), lambda i: (i, 0)),
            pl.BlockSpec((STRETCH, NSTATE), lambda i: (i, 0)),
            pl.BlockSpec((STRETCH, heads), lambda i: (i, 0)),
            pl.BlockSpec((NSTATE, width), lambda i: (0, 0)),
        ],
        out_specs=pl.BlockSpec((STRETCH, width), lambda i: (i, 0)),
        out_shape=jax.ShapeDtypeStruct((rows, width), BF16),
        name="finish",
    )(partial, c, long_col, incoming)


def shards(
    residual,
    expert_rows,
    expert_ids,
    expert_slots,
    combine_weights,
    norm_gain,
    in_weight,
    conv_weight,
    conv_bias,
    bc_weight,
    dt_weight,
    dt_bias,
    decay_log,
    skip_gain,
):
    own_rows, width = residual.shape
    members = lax.axis_size("exp")
    returned = lax.all_to_all(expert_rows, "exp", split_axis=2, concat_axis=1, tiled=True)
    capacity = returned.shape[3]
    slots = returned.shape[1] * capacity
    buffers = returned.reshape(slots, width)
    index = expert_ids * capacity + expert_slots
    chosen = index[:, :, None] == jnp.arange(slots, dtype=jnp.int32)[None, None, :]
    weights = jnp.sum(jnp.where(chosen, combine_weights[:, :, None], 0.0), axis=1)
    high = lax.reduce_precision(weights, 8, 7)
    normed = combine(
        high.astype(BF16), (weights - high).astype(BF16), buffers, residual, norm_gain[None, :]
    )
    group_rows = own_rows * members
    local_width = in_weight.shape[1]
    piece = own_rows // CHUNKS
    products = []
    for turn in range(CHUNKS):
        gathered = lax.all_gather(
            normed[turn * piece : (turn + 1) * piece], "exp", axis=0, tiled=True
        )
        products.append(mm(gathered, in_weight).astype(BF16).reshape(members, piece, local_width))
    x_in = jnp.stack(products, axis=1).reshape(group_rows, local_width)

    count = lax.axis_size("seq")
    rim_rows = lax.ppermute(
        x_in[group_rows - (KCONV - 1) :], "seq", [(s, s + 1) for s in range(count - 1)]
    )
    padded = jnp.concatenate([rim_rows, x_in], axis=0)
    filtered = jnp.zeros((group_rows, local_width), F32) + conv_bias[None, :]
    for tap in range(KCONV):
        filtered = filtered + conv_weight[tap][None, :] * padded[tap : tap + group_rows].astype(F32)
    activated = jax.nn.silu(filtered).astype(BF16)

    heads = local_width // HEAD
    state_width = bc_weight.shape[1] // members
    projections = jnp.concatenate(
        [
            bc_weight.reshape(local_width, members, state_width),
            dt_weight.reshape(local_width, members, heads),
        ],
        axis=2,
    ).reshape(local_width, members * (state_width + heads))
    parts = lax.dot_general(
        projections, activated, (((0,), (1,)), ((), ())), preferred_element_type=F32
    ).astype(BF16)
    parts = parts.reshape(members, state_width + heads, group_rows)
    parts = lax.all_to_all(parts, "exp", split_axis=0, concat_axis=0, tiled=True)
    sums = jnp.sum(parts.astype(F32), axis=0)
    maps = lax.all_gather(sums[:state_width].astype(BF16), "exp", axis=0, tiled=True)
    b_t = maps[:NSTATE]
    c = maps[NSTATE:].T
    dt_row = jax.nn.softplus(sums[state_width:] + dt_bias[:, None])
    blocks = group_rows // STRETCH
    decays = (-jnp.exp(decay_log)[:, None] * dt_row).reshape(heads, blocks, STRETCH)
    running = jnp.cumsum(decays, axis=2)
    totals = running[:, :, -1]
    before = jnp.cumsum(totals, axis=1) - totals
    row = running.reshape(heads, group_rows)
    col = row.T
    long_col = (running + before[:, :, None]).reshape(heads, group_rows).T
    span = jnp.sum(totals, axis=1)

    starts, final = states_of(activated, b_t, row, dt_row, col)
    extra = jnp.broadcast_to(jnp.repeat(span, HEAD)[None, :], (8, local_width))
    everyone = lax.all_gather(jnp.concatenate([final, extra], axis=0), "seq", axis=0)
    partial = inside_of(
        activated, b_t, c, row, dt_row, col, starts, jnp.repeat(skip_gain, HEAD)[None, :]
    )
    here = lax.axis_index("seq")
    order = jnp.arange(count)
    spans = everyone[:, NSTATE, :]
    between = (order[None, :] > order[:, None]) & (order[None, :] < here)
    gaps = jnp.sum(jnp.where(between[:, :, None], spans[None, :, :], 0.0), axis=1)
    shares = jnp.where((order < here)[:, None], jnp.exp(gaps), 0.0)
    incoming = jnp.sum(shares[:, None, :] * everyone[:, :NSTATE, :], axis=0)
    return finish(partial, c, long_col, incoming)


def solution(mesh):
    placed = (
        P(("seq", "exp"), None),
        P("seq", "exp", None, None, None),
        P(("seq", "exp"), None),
        P(("seq", "exp"), None),
        P(("seq", "exp"), None),
        P(),
        P(None, "exp"),
        P(None, "exp"),
        P("exp"),
        P("exp", None),
        P("exp", None),
        P("exp"),
        P("exp"),
        P("exp"),
    )
    return jax.shard_map(
        shards, mesh=mesh, in_specs=placed, out_specs=P("seq", "exp"), check_vma=False
    )
```

time: 615 us -> 488 us (0.79)
  blocking collectives: 75.8 us -> 16.9 us
  local copies, waits for them, and re-layouts: 52.2 us -> 8.81 us
  starting transfers between devices: 54.8 us -> 16.8 us
  Pallas kernels: 0 us -> 35.2 us
  other arithmetic: 41.4 us -> 16.1 us
  waiting for transfers between devices: 329 us -> 348 us
  matrix products: 46.7 us -> 31.2 us
    psum x1 -> x0, blocking collectives: 75.8 us -> none  [shards(): state_proj, dt_raw = lax.psum((state_part, rate_part), 'exp')]
    ppermute x8 -> x1, starting transfers between devices: 46.9 us -> 3.91 us  [shards(): lax.ppermute(x_in[group_rows - (KCONV - 1):], 'seq', [(s, s + 1) for s in...]
    pallas_call x0 -> x4, Pallas kernels: none -> 35.2 us  [the longest x1 10.5 us: inside_of(): pl.pallas_call(inside_body, grid=(rows // STRETCH,), in_specs=[pl.BlockSp...]
    all_gather x1 -> x3, waiting for transfers between devices: 207 us -> 232 us  [the longest x2 218 us: shards(): lax.all_gather(normed[turn * piece:(turn + 1) * piece], 'exp', axis=0, ti...]
    ppermute x8 -> x1, waiting for transfers between devices: 23.7 us -> 0.71 us  [shards(): lax.ppermute(x_in[group_rows - (KCONV - 1):], 'seq', [(s, s + 1) for s in...]
    gather x2 -> x0, local copies, waits for them, and re-layouts: 20.2 us -> none  [shards(): picked = jnp.take(buffers, expert_ids * capacity + expert_slots, axis=0)]
    all_to_all x0 -> x1, waiting for transfers between devices: none -> 17.3 us  [shards(): lax.all_to_all(parts, 'exp', split_axis=0, concat_axis=0, tiled=True)]
    all_gather x0 -> x1, blocking collectives: none -> 16.9 us  [shards(): lax.all_gather(sums[:state_width].astype(BF16), 'exp', axis=0, tiled=True)]
  transfers between devices with their start and end apart: 11 -> 6, of which waited for: 10 -> 6; matrix products, arithmetic and copies ran while one was open for 2% -> 4% of each run, Pallas kernels for 0% -> 2%
where the time goes in v1:
time: 488 us; the launch traced here: 487 us
  waiting for transfers between devices  348 us (71%)
  Pallas kernels  35.2 us (7%)
  matrix products  31.2 us (6%)
  blocking collectives  16.9 us (3%)
  starting transfers between devices  16.8 us (3%)
  other arithmetic  16.1 us (3%)
  between operations  13.5 us (3%)
  local copies, waits for them, and re-layouts  8.81 us (2%)
    all_gather x2, waiting for transfers between devices, shards(): lax.all_gather(normed[turn * piece:(turn + 1) * piece], 'exp', axis=0, ti...  218 us
    all_to_all x1, waiting for transfers between devices, shards(): lax.all_to_all(expert_rows, 'exp', split_axis=2, concat_axis=1, tiled=True)  97.7 us
    dot_general x2, matrix products, mm(): return jnp.dot(a, b, preferred_element_type=F32)  29.5 us
    all_to_all x1, waiting for transfers between devices, shards(): lax.all_to_all(parts, 'exp', split_axis=0, concat_axis=0, tiled=True)  17.3 us
    all_gather x1, blocking collectives, shards(): lax.all_gather(sums[:state_width].astype(BF16), 'exp', axis=0, tiled=True)  16.9 us
    all_gather x1, waiting for transfers between devices, shards(): lax.all_gather(jnp.concatenate([final, extra], axis=0), 'seq', axis=0)  13.9 us
    pallas_call x1, Pallas kernels, inside_of(): pl.pallas_call(inside_body, grid=(rows // STRETCH,), in_specs=[pl.BlockSp...  10.5 us
    pallas_call x1, Pallas kernels, combine(): pl.pallas_call(combine_body, grid=(width // part,), in_specs=[pl.BlockSpe...  9.78 us
  transfers between devices with their start and end apart: 6, of which 6 were waited for; matrix products, arithmetic and copies ran while one was open for 4% of the time, Pallas kernels for 2%

profile of v1, /device:TPU:1, one launch (start us, length us, event | category | flops | bytes accessed | tf_op | source)
XLA Modules:
  0.0 486.9 jit_solution(15239968973429906949)
XLA Ops:
  6.5 7.7 %all-to-all-start = ((bf16[1,1,16,24,8192]{4,3,1,0,2:T(8,128)(2,1)}), bf16[1,1,16,24,8192]{4,3,1,0,2:T(8,128)(2,1)}, u32[]{:S(2)}, u32[]{:S(2)}) async-start(bf16[1,1,16,24,8192]{4,3,1,0,2:T(8,128)(2,1)} %bitcast.48), calls=%async_computation | async-start | bytes 12582912 | tf_op jit(solution)/shard_map/all_to_all | solution.py:240
  14.3 0.0 all-gather.5.cloned.1.call-start
  14.3 0.0 copy-done.7
  14.4 0.0 copy-done.8
  14.4 0.1 select_reduce_fusion
  14.5 0.7 fusion.3
  15.2 97.7 %all-to-all-done = bf16[1,1,16,24,8192]{4,3,1,0,2:T(8,128)(2,1)} async-done(((bf16[1,1,16,24,8192]{4,3,1,0,2:T(8,128)(2,1)}), bf16[1,1,16,24,8192]{4,3,1,0,2:T(8,128)(2,1)}, u32[]{:S(2)}, u32[]{:S(2)}) %all-to-all-start) | async-done | bytes 6291488 | tf_op jit(solution)/shard_map/all_to_all | solution.py:240
  112.9 9.8 %combine.1 = bf16[128,8192]{1,0:T(8,128)(2,1)} custom-call(bf16[128,384]{1,0:T(8,128)(2,1)} %get-tuple-element.16.hi_ref, bf16[128,384]{1,0:T(8,128)(2,1)} %get-tuple-element.15.lo_ref, bf16[384,8192]{1,0:T(8,128)(2,1)} %bitcast.2.rows_ref, bf16[128,8192]{1,0:T(8,128)(2,1)} %residual_ref.1, f32[1,8192]{1,0:T(1,128)} %bitcast.62), custom_call_target="tpu_custom_call" | custom-call | tf_op jit(solution)/shard_map/combine/pallas_call | solution.py:51
  122.7 3.1 fusion.7
  125.7 0.0 all-gather.5.cloned.1.call-update
  125.8 0.0 all-gather.7.cloned.1.call-start
  125.8 0.7 all-gather.7.cloned.1.call-update
  126.5 0.0 copy-done.2
  126.5 0.1 copy.82
  126.7 0.1 copy.83
  126.8 120.0 %all-gather.5.cloned.1.call-done = bf16[1024,8192]{1,0:T(8,128)(2,1)} async-done(((bf16[64,8192]{1,0:T(8,128)(2,1)}), bf16[1024,8192]{1,0:T(8,128)(2,1)}) %all-gather.5.cloned.1.call-update) | async-done | bytes 16777232 | tf_op jit(solution)/shard_map/all_gather | solution.py:256
  246.8 14.8 %convolution_convert_fusion.2 = bf16[1024,512]{1,0:T(8,128)(2,1)S(1)} fusion(bf16[1024,8192]{1,0:T(8,128)(2,1)} %all-gather.5.cloned.1.call-done, bf16[8192,512]{1,0:T(8,128)(2,1)} %param.20), kind=kOutput, calls=%fused_computation.10 | convolution fusion | flops 8590458880 | bytes 26214400 | tf_op jit(solution)/shard_map/dot_general | solution.py:19
  261.5 98.2 %all-gather.7.cloned.1.call-done = bf16[1024,8192]{1,0:T(8,128)(2,1)} async-done(((bf16[64,8192]{1,0:T(8,128)(2,1)}), bf16[1024,8192]{1,0:T(8,128)(2,1)}) %all-gather.7.cloned.1.call-update) | async-done | bytes 16777232 | tf_op jit(solution)/shard_map/all_gather | solution.py:256
  359.7 14.8 %convolution_convert_fusion.1 = bf16[1024,512]{1,0:T(8,128)(2,1)S(1)} fusion(bf16[1024,8192]{1,0:T(8,128)(2,1)} %all-gather.7.cloned.1.call-done, bf16[8192,512]{1,0:T(8,128)(2,1)} %param.20), kind=kOutput, calls=%fused_computation.9 | convolution fusion | flops 8590458880 | bytes 26214400 | tf_op jit(solution)/shard_map/dot_general | solution.py:19
  374.5 0.0 copy-start.5
  374.5 0.2 pad_maximum_fusion.1
  374.7 3.9 collective-permute-start
  378.7 0.7 collective-permute-done
  379.4 0.0 copy-done.5
  379.4 3.0 multiply_convert_fusion.values_ref
  382.4 0.0 copy-start
  382.4 0.0 copy-start.9
  382.4 1.7 convolution_convert_fusion
  384.1 5.0 %all-to-all-start.1 = ((bf16[16,16,2048]{2,1,0:T(8,128)(2,1)}), bf16[16,16,2048]{2,1,0:T(8,128)(2,1)S(1)}, u32[]{:S(2)}, u32[]{:S(2)}) async-start(bf16[16,16,2048]{2,1,0:T(8,128)(2,1)} %bitcast.50), calls=%async_computation.1 | async-start | bytes 2097152 | tf_op jit(solution)/shard_map/all_to_all | solution.py:285
  389.1 0.0 all-gather.9.cloned.1.call-start
  389.2 17.3 %all-to-all-done.1 = bf16[16,16,2048]{2,1,0:T(8,128)(2,1)S(1)} async-done(((bf16[16,16,2048]{2,1,0:T(8,128)(2,1)}), bf16[16,16,2048]{2,1,0:T(8,128)(2,1)S(1)}, u32[]{:S(2)}, u32[]{:S(2)}) %all-to-all-start.1) | async-done | bytes 1048608 | tf_op jit(solution)/shard_map/all_to_all | solution.py:285
  406.5 0.1 convert_reduce_fusion
  406.7 0.7 broadcast_multiply_fusion
  407.4 4.5 reduce-window.6
  412.0 0.1 slice.88
  412.0 0.2 copy.86
  412.2 0.1 fusion.4
  412.3 0.0 copy-start.10
  412.3 0.1 fusion.16
  412.4 0.1 broadcast_add_fusion
  412.5 0.1 slice.90
  412.6 0.2 slice_reduce_fusion
  412.8 0.1 broadcast_in_dim.81
  412.9 0.1 broadcast_in_dim.82
  413.0 0.3 copy.88
  413.3 0.0 copy-done
  413.3 1.0 copy.90.row_ref
  414.4 16.9 %all_gather.17 = bf16[128,2048]{1,0:T(8,128)(2,1)S(1)} all-gather(bf16[8,2048]{1,0:T(8,128)(2,1)S(1)} %slice.114), channel_id=1, replica_groups=mesh['seq'=8,'exp'=16] {'exp'}, dimensions={0}, use_global_device_ids=true | all-gather | bytes 557056 | tf_op jit(solution)/shard_map/all_gather | solution.py:287
  431.2 0.8 fusion.8
  432.0 7.2 %states.1 = (f32[8,64,512]{2,1,0:T(8,128)}, f32[64,512]{1,0:T(8,128)}) custom-call(bf16[2048,512]{1,0:T(8,128)(2,1)} %copy-done, bf16[64,2048]{1,0:T(8,128)(2,1)} %get-tuple-element.14.b_ref, f32[8,2048]{1,0:T(8,128)} %copy.90.row_ref, f32[8,2048]{1,0:T(8,128)} %get-tuple-element.10.dt_ref, f32[2048,8]{1,0:T(8,128)} %bitcast.44), custom_call_target="tpu_custom_call" | custom-call | tf_op jit(solution)/shard_map/states/pallas_call | solution.py:112
  439.2 1.6 pad_maximum_fusion.3
  440.8 0.0 all-gather.9.cloned.1.call-update
  440.8 0.1 broadcast_in_dim.78
  440.9 0.6 broadcast_in_dim_reshape.4.skip_ref
  441.6 0.1 copy.92
  441.7 2.3 bitcast_add_fusion
  444.0 1.1 copy.94
  445.1 10.5 %inside.1.partial_ref = f32[2048,512]{1,0:T(8,128)} custom-call(bf16[2048,512]{1,0:T(8,128)(2,1)} %copy-done, bf16[64,2048]{1,0:T(8,128)(2,1)} %get-tuple-element.14.b_ref, bf16[2048,64]{1,0:T(8,128)(2,1)} %bitcast.51, f32[8,2048]{1,0:T(8,128)} %copy.90.row_ref, f32[8,2048]{1,0:T(8,128)} %get-tuple-element.10.dt_ref, f32[2048,8]{1,0:T(8,128)} %bitcast.45, ...), custom_call_target="tpu_custom_call" | custom-call | flops 10737418240 | bytes 8388608 | tf_op jit(solution)/shard_map/inside/pallas_call | solution.py:166
  455.6 13.9 %all-gather.9.cloned.1.call-done = f32[576,512]{1,0:T(8,128)} async-done(((f32[72,512]{1,0:T(8,128)}), f32[576,512]{1,0:T(8,128)}) %all-gather.9.cloned.1.call-update) | async-done | bytes 1179664 | tf_op jit(solution)/shard_map/all_gather | solution.py:303
  469.5 0.9 slice.91
  470.4 0.1 select_reduce_fusion.1
  470.5 0.1 exponential_select_fusion
  470.6 2.0 fusion.2.incoming_ref
  472.6 7.7 %finish.1 = bf16[2048,512]{1,0:T(8,128)(2,1)} custom-call(f32[2048,512]{1,0:T(8,128)} %inside.1.partial_ref, bf16[2048,64]{1,0:T(8,128)(2,1)} %bitcast.52, f32[2048,8]{1,0:T(8,128)} %bitcast.49, f32[64,512]{1,0:T(8,128)} %fusion.2.incoming_ref), custom_call_target="tpu_custom_call" | custom-call | tf_op jit(solution)/shard_map/finish/pallas_call | solution.py:207
  (29 shorter events, 0.2 us)
Async XLA Ops:
  6.5 7.8 %copy-start.7 = (s32[128,2]{0,1:T(2,128)S(1)}, s32[128,2]{0,1:T(2,128)}, u32[]{:S(2)}) copy-start(s32[128,2]{0,1:T(2,128)} %param.17) | copy-start | bytes 3076
  6.5 7.8 %copy-start.8 = (s32[128,2]{0,1:T(2,128)S(1)}, s32[128,2]{0,1:T(2,128)}, u32[]{:S(2)}) copy-start(s32[128,2]{0,1:T(2,128)} %param.16) | copy-start | bytes 3076
  6.5 7.8 %copy-start.6 = (f32[128,2]{0,1:T(2,128)S(1)}, f32[128,2]{0,1:T(2,128)}, u32[]{:S(2)}) copy-start(f32[128,2]{0,1:T(2,128)} %param.18) | copy-start | bytes 3076
  6.5 106.3 %all-to-all-start = ((bf16[1,1,16,24,8192]{4,3,1,0,2:T(8,128)(2,1)}), bf16[1,1,16,24,8192]{4,3,1,0,2:T(8,128)(2,1)}, u32[]{:S(2)}, u32[]{:S(2)}) async-start(bf16[1,1,16,24,8192]{4,3,1,0,2:T(8,128)(2,1)} %bitcast.48), calls=%async_computation | async-start | bytes 12582912 | tf_op jit(solution)/shard_map/all_to_all | solution.py:240
  14.3 232.5 %all-gather.5.cloned.1.call-start = ((), (), s32[]{:S(2)}) async-start(), calls=%async_computation.2 | async-start | bytes 17825792 | tf_op jit(solution)/shard_map/all_gather | solution.py:256
  122.7 3.9 copy-start.2
  122.7 4.0 copy-start.3
  122.7 4.1 copy-start.4
  125.8 233.9 %all-gather.7.cloned.1.call-start = ((), (), s32[]{:S(2)}) async-start(), calls=%async_computation.3 | async-start | bytes 17825792 | tf_op jit(solution)/shard_map/all_gather | solution.py:256
  374.5 4.9 %copy-start.5 = (f32[512]{0:T(512)S(1)}, f32[512]{0:T(512)}, u32[]{:S(2)}) copy-start(f32[512]{0:T(512)} %param.22) | copy-start | bytes 6148
  374.7 4.6 collective-permute-start
  379.4 9.8 %copy-start.11 = (f32[8]{0:T(128)S(1)}, f32[8]{0:T(128)}, u32[]{:S(2)}) copy-start(f32[8]{0:T(128)} %param.26) | copy-start | bytes 100
  382.4 30.9 %copy-start = (bf16[2048,512]{1,0:T(8,128)(2,1)}, bf16[2048,512]{1,0:T(8,128)(2,1)S(1)}, u32[]{:S(2)}) copy-start(bf16[2048,512]{1,0:T(8,128)(2,1)S(1)} %multiply_convert_fusion.values_ref) | copy-start | bytes 6291460
  382.4 24.2 %copy-start.9 = (f32[8]{0:T(128)S(1)}, f32[8]{0:T(128)}, u32[]{:S(2)}) copy-start(f32[8]{0:T(128)} %param.25) | copy-start | bytes 100
  384.1 22.4 %all-to-all-start.1 = ((bf16[16,16,2048]{2,1,0:T(8,128)(2,1)}), bf16[16,16,2048]{2,1,0:T(8,128)(2,1)S(1)}, u32[]{:S(2)}, u32[]{:S(2)}) async-start(bf16[16,16,2048]{2,1,0:T(8,128)(2,1)} %bitcast.50), calls=%async_computation.1 | async-start | bytes 2097152 | tf_op jit(solution)/shard_map/all_to_all | solution.py:285
  389.1 80.3 %all-gather.9.cloned.1.call-start = ((), (), s32[]{:S(2)}) async-start(), calls=%async_computation.4 | async-start | bytes 1327104 | tf_op jit(solution)/shard_map/all_gather | solution.py:303
  412.3 28.5 %copy-start.10 = (f32[8]{0:T(128)S(1)}, f32[8]{0:T(128)}, u32[]{:S(2)}) copy-start(f32[8]{0:T(128)} %param.27) | copy-start | bytes 100
  413.3 18.7 %copy-start.1 = (f32[8,8,2,128]{0,3,2,1:T(8,128)}, f32[8,8,2,128]{0,3,2,1:T(8,128)S(1)}, u32[]{:S(2)}) copy-start(f32[8,8,2,128]{0,3,2,1:T(8,128)S(1)} %copy.88) | copy-start | bytes 196612
Sparse Core Ops, SparseCore 0:
  125.9 120.8 all-gather.4
  248.9 110.7 all-gather.6
  440.9 28.4 all-gather.8
